TPU v7x, 32 devices: a whole 2x2x4 slice. The times are simulated.
32 devices in a mesh: fsdp: 8 (over z, core), tp: 4 (over y, x).
Axes of the slice: x: 2, y: 2, z: 4, core: 2. Of those that a mesh axis runs over, the one named last changes fastest.
Arguments:
- hidden: bfloat16 [8192, 14336], P('fsdp', 'tp'), may hold values from -6 to 6
- grad_out: bfloat16 [8192, 4096], P('fsdp'), may hold values from -0.09375 to 0.09375
- master: float32 [4096, 14336], P('fsdp', 'tp'), may hold values from -0.046875 to 0.046875
- moment_one: float32 [4096, 14336], P('fsdp', 'tp'), may hold values from -3 to 3
- moment_two: float32 [4096, 14336], P('fsdp', 'tp'), may hold values from 0.1 to 4
Outputs:
- new_master: float32 [4096, 14336], P('fsdp', 'tp')
- new_one: float32 [4096, 14336], P('fsdp', 'tp')
- new_two: float32 [4096, 14336], P('fsdp', 'tp')
- quantized: bfloat16 [4096, 14336], P(None, 'fsdp')
- block_scales: bfloat16 [32, 112], P(None, 'fsdp')
All inputs are finite; a program needn't handle non-finite values.
Results may differ from a plain program's by a relative error of at most 0.0051.
Values may be sent and summed in bfloat16 or wider, within the bound.
No kernel may reach another device: no remote copies, remote signals or barrier semaphores. Data moves between devices by JAX's collectives and lax.ppermute only.
A program may use at most 192 MiB of HBM per device.

v0:
```python
import jax
import jax.numpy as jnp
from jax import lax
from jax.sharding import PartitionSpec as P

BLOCK = 128


beta_one = 0.9
beta_two = 0.95
learn_rate = 0.005
adam_eps = 1e-08
scale_eps = 1e-06
steps_done = 4


def quantize(weights):
    rows, cols = weights.shape
    blocks = weights.reshape(rows // BLOCK, BLOCK, cols // BLOCK, BLOCK)
    peak = jnp.max(jnp.abs(blocks), axis=(1, 3)) + scale_eps
    scales = peak.astype(jnp.bfloat16)
    widened = lax.optimization_barrier(scales).astype(jnp.float32)
    values = (blocks / widened[:, None, :, None]).reshape(rows, cols).astype(jnp.bfloat16)
    return (values, scales)


def contract_tokens(left, right):
    return lax.dot_general(
        left, right, (((0,), (0,)), ((), ())), preferred_element_type=jnp.float32
    )


def local(hidden, grad_out, master, moment_one, moment_two):
    grad = lax.psum_scatter(
        contract_tokens(grad_out, hidden).astype(jnp.bfloat16),
        "fsdp",
        scatter_dimension=0,
        tiled=True,
    ).astype(jnp.float32)
    new_one = beta_one * moment_one + (1.0 - beta_one) * grad
    new_two = beta_two * moment_two + (1.0 - beta_two) * grad * grad
    fix_one = 1.0 - beta_one**steps_done
    fix_two = 1.0 - beta_two**steps_done
    new_master = master - learn_rate * (new_one / fix_one) / (
        jnp.sqrt(new_two / fix_two) + adam_eps
    )
    values, scales = quantize(new_master)
    wide_values, wide_scales = (
        lax.all_gather(values, "tp", axis=1, tiled=True),
        lax.all_gather(scales, "tp", axis=1, tiled=True),
    )
    quantized, block_scales = (
        lax.all_to_all(wide_values, "fsdp", split_axis=1, concat_axis=0, tiled=True),
        lax.all_to_all(wide_scales, "fsdp", split_axis=1, concat_axis=0, tiled=True),
    )
    return (new_master, new_one, new_two, quantized, block_scales)


def solution(mesh):
    return jax.shard_map(
        local,
        mesh=mesh,
        in_specs=(
            P("fsdp", "tp"),
            P("fsdp", None),
            P("fsdp", "tp"),
            P("fsdp", "tp"),
            P("fsdp", "tp"),
        ),
        out_specs=(
            P("fsdp", "tp"),
            P("fsdp", "tp"),
            P("fsdp", "tp"),
            P(None, "fsdp"),
            P(None, "fsdp"),
        ),
        check_vma=False,
    )
```

profile of v0, /device:TPU:0, one launch (start us, length us, event | category | flops | bytes accessed | tf_op | source)
XLA Modules:
  0.0 885.3 jit_solution(1451985399981447193)
XLA Ops:
  7.2 0.0 reduce-scatter.2.cloned.1.call-start
  7.2 38.1 %convolution_convert_fusion = bf16[4096,3584]{1,0:T(8,128)(2,1)} fusion(bf16[1024,4096]{1,0:T(8,128)(2,1)} %param.6, bf16[1024,3584]{1,0:T(8,128)(2,1)} %param.5), kind=kOutput, calls=%fused_computation | convolution fusion | flops 30079451136 | bytes 45088768 | tf_op jit(solution)/shard_map/dot_general | solution.py:28
  45.4 0.0 reduce-scatter.2.cloned.1.call-update
  45.4 0.2 all-gather.3.cloned.1.call-start
  45.6 289.2 %reduce-scatter.2.cloned.1.call-done = bf16[512,3584]{1,0:T(8,128)(2,1)} async-done(((bf16[4096,3584]{1,0:T(8,128)(2,1)}), bf16[512,3584]{1,0:T(8,128)(2,1)}) %reduce-scatter.2.cloned.1.call-update) | async-done | bytes 3670032 | tf_op jit(solution)/shard_map/reduce_scatter | solution.py:34
  334.8 19.4 %fusion.2 = (f32[512,3584]{1,0:T(8,128)}, f32[512,3584]{1,0:T(8,128)}, f32[512,3584]{1,0:T(8,128)}, f32[512,3584]{1,0:T(8,128)}) fusion(f32[512,3584]{1,0:T(8,128)} %param.7, bf16[512,3584]{1,0:T(8,128)(2,1)} %reduce-scatter.2.cloned.1.call-done, f32[512,3584]{1,0:T(8,128)} %param.8, f32[512,3584]{1,0:T(8,128)} %param.9), kind=kLoop, calls=%fused_computation.10 | loop fusion | flops 25690112 | bytes 55050240 | tf_op jit(solution)/shard_map/abs | solution.py:20
  354.3 9.3 %reshape.23 = f32[4,128,28,128]{3,2,1,0:T(8,128)} reshape(f32[512,3584]{1,0:T(8,128)} %get-tuple-element.15) | data formatting | bytes 14680064 | tf_op jit(solution)/shard_map/abs | solution.py:20
  363.6 4.2 reduce_max.9
  367.7 0.1 copy.26
  367.8 1.0 div.25
  368.9 3.9 copy.32
  372.8 8.4 copy.19
  381.2 8.3 divide_convert_fusion
  389.5 0.0 all-gather.3.cloned.1.call-update
  389.5 0.1 copy.21
  389.6 8.0 all-gather
  397.7 0.1 reshape.22
  397.8 0.1 all_to_all.32
  397.9 0.6 copy.23
  398.5 3.3 all-to-all-start.1
  401.8 126.2 %all-gather.3.cloned.1.call-done = bf16[512,14336]{1,0:T(8,128)(2,1)} async-done(((bf16[512,3584]{1,0:T(8,128)(2,1)}), bf16[512,14336]{1,0:T(8,128)(2,1)}) %all-gather.3.cloned.1.call-update) | async-done | bytes 14680080 | tf_op jit(solution)/shard_map/all_gather | solution.py:49
  528.0 13.1 %copy.31 = bf16[64,8,8,1792]{3,2,0,1:T(8,128)(2,1)} copy(bf16[64,8,8,1792]{3,2,1,0:T(8,128)(2,1)} %bitcast.28) | data formatting | bytes 29360128 | tf_op jit(solution)/shard_map/all_to_all | solution.py:53
  541.1 0.0 all-to-all-done.1
  541.1 5.5 all-to-all-start
  546.6 0.7 copy.24
  547.3 318.0 %all-to-all-done = bf16[512,8,1792]{2,0,1:T(8,128)(2,1)} async-done(((bf16[512,8,1792]{2,0,1:T(8,128)(2,1)}), bf16[512,8,1792]{2,0,1:T(8,128)(2,1)}, u32[]{:S(2)}, u32[]{:S(2)}) %all-to-all-start) | async-done | bytes 14680096 | tf_op jit(solution)/shard_map/all_to_all | solution.py:53
  865.3 13.1 %copy.34 = bf16[4096,1792]{1,0:T(8,128)(2,1)} copy(bf16[4096,1792]{1,0:T(8,128)(2,1)} %bitcast.1) | data formatting | bytes 29360128
  (3 shorter events, 0.0 us)
Async XLA Ops:
  7.2 327.6 %reduce-scatter.2.cloned.1.call-start = ((), (), s32[]{:S(2)}) async-start(), calls=%async_computation.3 | async-start | bytes 33030144 | tf_op jit(solution)/shard_map/reduce_scatter | solution.py:34
  45.4 482.6 %all-gather.3.cloned.1.call-start = ((), (), s32[]{:S(2)}) async-start(), calls=%async_computation.4 | async-start | bytes 18350080 | tf_op jit(solution)/shard_map/all_gather | solution.py:49
  398.5 142.6 %all-to-all-start.1 = ((bf16[4,8,14]{2,0,1:T(4,128)(2,1)}), bf16[4,8,14]{2,0,1:T(4,128)(2,1)S(1)}, u32[]{:S(2)}, u32[]{:S(2)}) async-start(bf16[4,8,14]{2,0,1:T(4,128)(2,1)} %copy.23), calls=%async_computation.2 | async-start | bytes 16384 | tf_op jit(solution)/shard_map/all_to_all | solution.py:54
  541.1 324.2 %all-to-all-start = ((bf16[512,8,1792]{2,0,1:T(8,128)(2,1)}), bf16[512,8,1792]{2,0,1:T(8,128)(2,1)}, u32[]{:S(2)}, u32[]{:S(2)}) async-start(bf16[512,8,1792]{2,0,1:T(8,128)(2,1)} %bitcast.25), calls=%async_computation.1 | async-start | bytes 29360128 | tf_op jit(solution)/shard_map/all_to_all | solution.py:53
Sparse Core Ops, SparseCore 0:
  45.5 289.2 reduce-scatter.1
  389.6 138.2 all-gather.2
where the time goes:
time: 886 us; the launch traced here: 885 us
  waiting for transfers between devices  733 us (83%)
  local copies, waits for them, and re-layouts  50.5 us (6%)
  matrix products  38.1 us (4%)
  other arithmetic  31.9 us (4%)
  between operations  14.1 us (2%)
  starting transfers between devices  9.13 us (1%)
    all_to_all x1, waiting for transfers between devices, local(): lax.all_to_all(wide_values, 'fsdp', split_axis=1, concat_axis=0, tiled=True)  318 us
    reduce_scatter x1, waiting for transfers between devices, local(): lax.psum_scatter(contract_tokens(grad_out, hidden).astype(jnp.bfloat16),...  289 us
    all_gather x1, waiting for transfers between devices, local(): lax.all_gather(values, 'tp', axis=1, tiled=True)  126 us
    dot_general x1, matrix products, contract_tokens(): lax.dot_general(left, right, (((0,), (0,)), ((), ())), preferred_element_...  38.1 us
    abs x1, other arithmetic, quantize(): peak = jnp.max(jnp.abs(blocks), axis=(1, 3)) + scale_eps  19.4 us
    unnamed x6, local copies, waits for them, and re-layouts  18 us
  transfers between devices with their start and end apart: 4, of which 3 were waited for; matrix products, arithmetic and copies ran while one was open for 2% of the time, Pallas kernels for 0%

commit v1 on v0

v1 whole, which is shorter than its diff:
```python
import functools
import itertools

import jax
import jax.numpy as jnp
from jax import lax
from jax.experimental import pallas as pl
from jax.experimental.pallas import tpu as pltpu
from jax.sharding import PartitionSpec as P


BLOCK = 128
SCALE_ROWS = 16

beta_one = 0.9
beta_two = 0.95
learn_rate = 0.005
adam_eps = 1e-08
scale_eps = 1e-06
steps_done = 4
fix_one = 1.0 - beta_one**steps_done
fix_two = 1.0 - beta_two**steps_done

AXES = ("fsdp", "tp")


def turn_kernel(table, source, target):
    target[0] = source[...].T


def turned(table, grad_out, rows):
    tokens, places = grad_out.shape[0], table.shape[0]
    return pl.pallas_call(
        turn_kernel,
        grid_spec=pltpu.PrefetchScalarGridSpec(
            num_scalar_prefetch=1,
            grid=(places,),
            in_specs=[pl.BlockSpec((tokens, rows), lambda s, tab: (0, tab[s]))],
            out_specs=pl.BlockSpec((1, rows, tokens), lambda s, tab: (s, 0, 0)),
        ),
        out_shape=jax.ShapeDtypeStruct((places, rows, tokens), grad_out.dtype),
        cost_estimate=pl.CostEstimate(flops=0, bytes_accessed=4 * tokens * places * rows, transcendentals=0),
        name="turn",
    )(table, grad_out)


def product_kernel(table, own_go, peer_go, own_lo, own_hi, peer_lo, peer_hi, sends, own, right):
    slot, last = pl.program_id(0), pl.num_programs(0) - 1
    width = own_lo.shape[1]

    @pl.when(slot == 0)
    def _():
        for which, (lo, hi) in enumerate(((own_lo, own_hi), (peer_lo, peer_hi))):
            right[which, :, :width] = lo[...]
            right[which, :, width:] = hi[...]

    total = jnp.dot(own_go[0], right[0], preferred_element_type=jnp.float32)
    total += jnp.dot(peer_go[0], right[1], preferred_element_type=jnp.float32)

    @pl.when(slot < last)
    def _():
        sends[0] = total.astype(sends.dtype)

    @pl.when(slot == last)
    def _():
        own[...] = total


def partial_products(at, table, grad_out, peer_grad, hidden, peer_hidden):
    j, chunks, width = at
    tokens, (places, rows) = hidden.shape[0], grad_out.shape[:2]
    lo, hi = lambda s, tab: (0, j), lambda s, tab: (0, chunks + j)
    turned_spec = pl.BlockSpec((1, rows, tokens), lambda s, tab: (tab[s], 0, 0))
    return pl.pallas_call(
        product_kernel,
        grid_spec=pltpu.PrefetchScalarGridSpec(
            num_scalar_prefetch=1,
            grid=(places,),
            in_specs=[
                turned_spec,
                turned_spec,
                pl.BlockSpec((tokens, width), lo),
                pl.BlockSpec((tokens, width), hi),
                pl.BlockSpec((tokens, width), lo),
                pl.BlockSpec((tokens, width), hi),
            ],
            out_specs=[
                pl.BlockSpec((1, rows, 2 * width), lambda s, tab: (jnp.minimum(s, places - 2), 0, 0)),
                pl.BlockSpec((rows, 2 * width), lambda s, tab: (0, 0)),
            ],
            scratch_shapes=[pltpu.VMEM((2, tokens, 2 * width), jnp.bfloat16)],
        ),
        out_shape=[
            jax.ShapeDtypeStruct((places - 1, rows, 2 * width), jnp.bfloat16),
            jax.ShapeDtypeStruct((rows, 2 * width), jnp.float32),
        ],
        cost_estimate=pl.CostEstimate(
            flops=8 * tokens * places * rows * width,
            bytes_accessed=4 * tokens * places * rows + 8 * tokens * width + 4 * places * rows * width,
            transcendentals=0,
        ),
        name="products",
    )(table, grad_out, peer_grad, hidden, hidden, peer_hidden, peer_hidden)


def adam_kernel(arrivals, core, own, *refs):
    others, refs = refs[:arrivals], refs[arrivals:]
    master, one, two = refs[:3]
    new_master, new_one, new_two, same, cross = refs[-5:]
    side, step = pl.program_id(0), pl.program_id(1)
    grad = own[...]
    for other in others:
        grad += other[0].astype(jnp.float32)
    first = beta_one * one[...] + (1.0 - beta_one) * grad
    second = beta_two * two[...] + (1.0 - beta_two) * grad * grad
    weights = master[...] - (learn_rate / fix_one) * first / (jnp.sqrt(second * (1.0 / fix_two)) + adam_eps)
    new_one[...] = first
    new_two[...] = second
    new_master[...] = weights
    height, width = weights.shape
    rows = same.shape[0] - SCALE_ROWS
    line = lax.broadcasted_iota(jnp.int32, (SCALE_ROWS, width), 0)

    def put(target):
        slab = target[rows:, :].astype(jnp.float32)
        for up in range(height // BLOCK):
            scales, values = [], []
            for across in range(width // BLOCK):
                block = weights[up * BLOCK : (up + 1) * BLOCK, across * BLOCK : (across + 1) * BLOCK]
                peak = jnp.max(jnp.max(jnp.abs(block), axis=0, keepdims=True), axis=1, keepdims=True)
                scale = (jnp.broadcast_to(peak, (1, BLOCK)) + scale_eps).astype(jnp.bfloat16).astype(jnp.float32)
                scales.append(scale)
                values.append((block * (1.0 / scale)).astype(jnp.bfloat16))
            at = step * height + up * BLOCK
            target[pl.ds(pl.multiple_of(at, BLOCK), BLOCK), :] = jnp.concatenate(values, axis=1)
            slab = jnp.where(line == at // BLOCK, jnp.concatenate(scales, axis=1), slab)
        target[rows:, :] = slab.astype(jnp.bfloat16)

    @pl.when(side == 0)
    def _():
        put(same)

    @pl.when(side == 1)
    def _():
        put(cross)


def adam(at, core, own, arrivals, master, one, two, before):
    j, chunks, width = at
    rows = own.shape[0]
    height = 2 * BLOCK if rows % (2 * BLOCK) == 0 else BLOCK
    side = lambda s, core: (core[0] + s) % 2
    state = pl.BlockSpec((height, width), lambda s, r, core: (r, side(s, core) * chunks + j))
    whole = jax.ShapeDtypeStruct(master.shape, jnp.float32)
    packed = jax.ShapeDtypeStruct((rows + SCALE_ROWS, width), jnp.bfloat16)
    packed_spec = pl.BlockSpec((rows + SCALE_ROWS, width), lambda s, r, core: (0, 0))
    count = len(arrivals)
    return pl.pallas_call(
        functools.partial(adam_kernel, count),
        grid_spec=pltpu.PrefetchScalarGridSpec(
            num_scalar_prefetch=1,
            grid=(2, rows // height),
            in_specs=[pl.BlockSpec((height, width), lambda s, r, core: (r, side(s, core)))]
            + [pl.BlockSpec((1, height, width), lambda s, r, core: (0, r, side(s, core)))] * count
            + [state] * 3
            + [pl.BlockSpec(memory_space=pl.ANY)] * len(before),
            out_specs=[state, state, state, packed_spec, packed_spec],
        ),
        out_shape=[whole, whole, whole, packed, packed],
        input_output_aliases={5 + count + i: i for i in range(len(before))},
        cost_estimate=pl.CostEstimate(
            flops=60 * rows * width, bytes_accessed=2 * rows * width * (30 + 2 * count), transcendentals=2 * rows * width
        ),
        name="adam",
    )(core, own, *arrivals, master, one, two, *before)


def place_kernel(count, table, core, *refs):
    pieces, (values, scales) = refs[:count], refs[-2:]
    rows = values.shape[0] // 2
    for k, piece in enumerate(pieces):

        @pl.when(pl.program_id(0) == k)
        def _():
            for i in range(2):
                spot = (core[0] + i) % 2
                values[pl.ds(pl.multiple_of(spot * rows, rows), rows), :] = piece[i, :rows, :]
                scales[spot] = piece[i, rows:, :]


def place(at, table, core, pieces, half, before):
    j, _, width = at
    count, (_, packed, _) = len(pieces), pieces[0].shape
    rows = packed - SCALE_ROWS
    return pl.pallas_call(
        functools.partial(place_kernel, count),
        grid_spec=pltpu.PrefetchScalarGridSpec(
            num_scalar_prefetch=2,
            grid=(count,),
            in_specs=[pl.BlockSpec((2, packed, width), lambda k, tab, core: (0, 0, 0))] * count
            + [pl.BlockSpec(memory_space=pl.ANY)] * len(before),
            out_specs=[
                pl.BlockSpec((2 * rows, width), lambda k, tab, core: (tab[k], j)),
                pl.BlockSpec((2, SCALE_ROWS, width), lambda k, tab, core: (tab[k], 0, j)),
            ],
        ),
        out_shape=[
            jax.ShapeDtypeStruct((2 * count * rows, half), jnp.bfloat16),
            jax.ShapeDtypeStruct((2 * count, SCALE_ROWS, half), jnp.bfloat16),
        ],
        input_output_aliases={2 + count + i: i for i in range(len(before))},
        cost_estimate=pl.CostEstimate(flops=0, bytes_accessed=8 * count * packed * width, transcendentals=0),
        name="place",
    )(table, core, *pieces, *before)


def cuts(blocks):
    sizes = [2] * (blocks // 2) + [1] * (blocks % 2)
    if blocks % 2 == 0:
        sizes[-1:] = [1, 1]
    chunks, start = [], 0
    for size in sizes:
        chunks.append((start // size, blocks // size, size * BLOCK))
        start += size
    return chunks


def plan(count, places):
    steps = []
    for i in range(min(2, count)):
        steps += [("product", i), ("hop", i, 0)]
    for i in range(count):
        steps.append(("hop", i, 1))
        if i >= 1:
            steps += [("adam", i - 1), ("plane", i - 1)]
        if i + 2 < count:
            steps += [("product", i + 2), ("hop", i + 2, 0)]
        steps += [("hop", i, k) for k in range(2, places - 1)]
        if i >= 2:
            steps.append(("gather", i - 2))
        if i >= 3:
            steps.append(("place", i - 3))
    steps += [("adam", count - 1), ("plane", count - 1)]
    for i in range(max(0, count - 2), count):
        steps.append(("gather", i))
        if i >= 1:
            steps.append(("place", i - 1))
    return steps + [("place", count - 1)]


def local(shards, groups, hidden, grad_out, master, moment_one, moment_two):
    places = shards // 2
    rows, half = master.shape[0], master.shape[1] // 2
    chunks = cuts(half // BLOCK)
    count = len(chunks)

    def permute(array, move):
        pairs = []
        for place, core, group in itertools.product(range(places), range(2), range(groups)):
            to = move(place, core, group)
            if to is not None:
                pairs.append(((place * 2 + core) * groups + group, (to[0] * 2 + to[1]) * groups + to[2]))
        return lax.ppermute(array, AXES, pairs)

    shard, group = lax.axis_index("fsdp"), lax.axis_index("tp")
    spot, core = shard // 2, shard % 2
    core_of = core.astype(jnp.int32).reshape(1)
    slots = jnp.arange(places)

    ahead = places - 1 - spot
    owner = jnp.where(slots < ahead, spot + 1 + slots, spot - 1 - (slots - ahead))
    owner = jnp.where(slots == places - 1, spot, owner).astype(jnp.int32)

    other_core = lambda p, c, t: (p, 1 - c, t)
    peer_hidden = permute(hidden, other_core)
    for_peer = turned((2 * slots + 1 - core).astype(jnp.int32), grad_out, rows)
    peer_grad = permute(for_peer, other_core)
    own_grad = turned((2 * slots + core).astype(jnp.int32), grad_out, rows)

    sends, own, arrivals, packed, pieces = {}, {}, {}, {}, {}
    state, shard_copy = [()], [()]

    def product(i):
        sends[i], own[i] = partial_products(chunks[i], owner, own_grad, peer_grad, hidden, peer_hidden)
        arrivals[i] = []

    def hop(i, k):
        payload = sends[i]
        if k:
            start = jnp.where(spot == k, 0, k)
            mine = lax.dynamic_slice_in_dim(payload, start, places - 1 - k, 0)
            payload = (mine.astype(jnp.float32) + arrivals[i][-1][1:].astype(jnp.float32)).astype(jnp.bfloat16)
        move = lambda p, c, t: (k + 1, c, t) if p == k else (places - 2 - k, c, t) if p == places - 1 - k else None
        arrivals[i].append(permute(payload, move))

    def update(i):
        *state[0], same, cross = adam(chunks[i], core_of, own[i], arrivals[i], master, moment_one, moment_two, state[0])
        packed[i] = (same, cross)

    def send(i):
        turn = i % groups
        same, cross = packed[i]
        packed[i] = (
            permute(same, lambda p, c, t: (t, c, p ^ turn)), permute(cross, lambda p, c, t: (t, 1 - c, p ^ turn))
        )

    def gather(i):
        both = jnp.stack(packed[i])
        pieces[i] = [both] + [permute(both, lambda p, c, t: (p, c, t ^ m)) for m in range(1, groups)]

    def put(i):
        sources = (group ^ slots ^ (i % groups)).astype(jnp.int32)
        shard_copy[0] = place(chunks[i], sources, core_of, pieces[i], half, shard_copy[0])

    actions = {"product": product, "hop": hop, "adam": update, "plane": send, "gather": gather, "place": put}
    for name, *where in plan(count, places):
        actions[name](*where)

    quantized, scales = shard_copy[0]
    lines, blocks = rows // BLOCK, half // BLOCK
    block_scales = scales[:, :lines].reshape(shards * lines, blocks, BLOCK)[:, :, 0]
    return (*state[0], quantized, block_scales)


def solution(mesh):
    shards, groups = mesh.shape["fsdp"], mesh.shape["tp"]
    assert shards == 2 * groups and groups & (groups - 1) == 0

    def body(*args):
        return local(shards, groups, *args)

    return jax.shard_map(
        body,
        mesh=mesh,
        in_specs=(
            P("fsdp", "tp"),
            P("fsdp", None),
            P("fsdp", "tp"),
            P("fsdp", "tp"),
            P("fsdp", "tp"),
        ),
        out_specs=(
            P("fsdp", "tp"),
            P("fsdp", "tp"),
            P("fsdp", "tp"),
            P(None, "fsdp"),
            P(None, "fsdp"),
        ),
        check_vma=False,
    )
```

time: 886 us -> 817 us (0.922)
  waiting for transfers between devices: 733 us -> 433 us
  starting transfers between devices: 9.13 us -> 191 us
  Pallas kernels: 0 us -> 163 us
  local copies, waits for them, and re-layouts: 50.5 us -> 6.02 us
  matrix products: 38.1 us -> 0 us
  other arithmetic: 31.9 us -> 18.9 us
  between operations: 14.1 us -> 1.64 us
    ppermute x0 -> x66, waiting for transfers between devices: none -> 433 us  [permute(): return lax.ppermute(array, AXES, pairs)]
    all_to_all x2 -> x0, waiting for transfers between devices: 318 us -> none  [the longest x1 318 us: local(): lax.all_to_all(wide_values, 'fsdp', split_axis=1, concat_axis=0, tiled=True)]
    reduce_scatter x1 -> x0, waiting for transfers between devices: 289 us -> none  [local(): lax.psum_scatter(contract_tokens(grad_out, hidden).astype(jnp.bfloat16),...]
    ppermute x0 -> x66, starting transfers between devices: none -> 191 us  [permute(): return lax.ppermute(array, AXES, pairs)]
    pallas_call x0 -> x26, Pallas kernels: none -> 163 us  [the longest x8 75.5 us: partial_products(): pl.pallas_call(product_kernel, grid_spec=pltpu.PrefetchScalarGridSpec(num...]
    all_gather x1 -> x0, waiting for transfers between devices: 126 us -> none  [local(): lax.all_gather(values, 'tp', axis=1, tiled=True)]
    dot_general x1 -> x0, matrix products: 38.1 us -> none  [contract_tokens(): lax.dot_general(left, right, (((0,), (0,)), ((), ())), preferred_element_...]
    abs x1 -> x0, other arithmetic: 19.4 us -> none  [quantize(): peak = jnp.max(jnp.abs(blocks), axis=(1, 3)) + scale_eps]
  transfers between devices with their start and end apart: 4 -> 66, of which waited for: 3 -> 30; matrix products, arithmetic and copies ran while one was open for 2% -> 2% of each run, Pallas kernels for 0% -> 18%
where the time goes in v1:
time: 817 us; the launch traced here: 814 us
  waiting for transfers between devices  433 us (53%)
  starting transfers between devices  191 us (23%)
  Pallas kernels  163 us (20%)
  other arithmetic  18.9 us (2%)
    ppermute x66, waiting for transfers between devices, permute(): return lax.ppermute(array, AXES, pairs)  433 us
    ppermute x66, starting transfers between devices, permute(): return lax.ppermute(array, AXES, pairs)  191 us
    pallas_call x8, Pallas kernels, partial_products(): pl.pallas_call(product_kernel, grid_spec=pltpu.PrefetchScalarGridSpec(num...  75.5 us
    pallas_call x8, Pallas kernels, adam(): pl.pallas_call(functools.partial(adam_kernel, count), grid_spec=pltpu.Pre...  44 us
    pallas_call x8, Pallas kernels, place(): pl.pallas_call(functools.partial(place_kernel, count), grid_spec=pltpu.Pr...  31.8 us
  transfers between devices with their start and end apart: 66, of which 30 were waited for; matrix products, arithmetic and copies ran while one was open for 2% of the time, Pallas kernels for 18%

profile of v1, /device:TPU:0, one launch (start us, length us, event | category | flops | bytes accessed | tf_op | source)
XLA Modules:
  0.0 813.8 jit_solution(13310874287572399133)
XLA Ops:
  1.7 5.9 turn.3
  8.2 5.9 turn.2.own_go
  14.6 4.2 collective-permute-done.peer_go
  18.8 7.7 products.8
  26.5 5.8 collective-permute-start.2
  32.3 7.7 products.9
  42.2 10.0 %products.10 = (bf16[3,512,512]{2,1,0:T(8,128)(2,1)}, f32[512,512]{1,0:T(8,128)}) custom-call(s32[4]{0:T(128)} %compare_select_fusion.1.table, bf16[4,512,1024]{2,1,0:T(8,128)(2,1)} %turn.2.own_go, bf16[4,512,1024]{2,1,0:T(8,128)(2,1)} %collective-permute-done.peer_go, bf16[1024,3584]{1,0:T(8,128)(2,1)} %own_hi.15, bf16[1024,3584]{1,0:T(8,128)(2,1)} %own_hi.15, ...), custom_call_target="tpu_custom_call" | custom-call | flops 4294967296 | bytes 12582912 | tf_op jit(solution)/shard_map/products/pallas_call | solution.py:74
  53.5 10.1 %products.11 = (bf16[3,512,512]{2,1,0:T(8,128)(2,1)}, f32[512,512]{1,0:T(8,128)}) custom-call(s32[4]{0:T(128)} %compare_select_fusion.1.table, bf16[4,512,1024]{2,1,0:T(8,128)(2,1)} %turn.2.own_go, bf16[4,512,1024]{2,1,0:T(8,128)(2,1)} %collective-permute-done.peer_go, bf16[1024,3584]{1,0:T(8,128)(2,1)} %own_hi.15, bf16[1024,3584]{1,0:T(8,128)(2,1)} %own_hi.15, ...), custom_call_target="tpu_custom_call" | custom-call | flops 4294967296 | bytes 12582912 | tf_op jit(solution)/shard_map/products/pallas_call | solution.py:74
  65.0 10.0 %products.13 = (bf16[3,512,512]{2,1,0:T(8,128)(2,1)}, f32[512,512]{1,0:T(8,128)}) custom-call(s32[4]{0:T(128)} %compare_select_fusion.1.table, bf16[4,512,1024]{2,1,0:T(8,128)(2,1)} %turn.2.own_go, bf16[4,512,1024]{2,1,0:T(8,128)(2,1)} %collective-permute-done.peer_go, bf16[1024,3584]{1,0:T(8,128)(2,1)} %own_hi.15, bf16[1024,3584]{1,0:T(8,128)(2,1)} %own_hi.15, ...), custom_call_target="tpu_custom_call" | custom-call | flops 4294967296 | bytes 12582912 | tf_op jit(solution)/shard_map/products/pallas_call | solution.py:74
  77.4 10.1 %products.12 = (bf16[3,512,512]{2,1,0:T(8,128)(2,1)}, f32[512,512]{1,0:T(8,128)}) custom-call(s32[4]{0:T(128)} %compare_select_fusion.1.table, bf16[4,512,1024]{2,1,0:T(8,128)(2,1)} %turn.2.own_go, bf16[4,512,1024]{2,1,0:T(8,128)(2,1)} %collective-permute-done.peer_go, bf16[1024,3584]{1,0:T(8,128)(2,1)} %own_hi.15, bf16[1024,3584]{1,0:T(8,128)(2,1)} %own_hi.15, ...), custom_call_target="tpu_custom_call" | custom-call | flops 4294967296 | bytes 12582912 | tf_op jit(solution)/shard_map/products/pallas_call | solution.py:74
  87.5 10.0 %products.14 = (bf16[3,512,512]{2,1,0:T(8,128)(2,1)}, f32[512,512]{1,0:T(8,128)}) custom-call(s32[4]{0:T(128)} %compare_select_fusion.1.table, bf16[4,512,1024]{2,1,0:T(8,128)(2,1)} %turn.2.own_go, bf16[4,512,1024]{2,1,0:T(8,128)(2,1)} %collective-permute-done.peer_go, bf16[1024,3584]{1,0:T(8,128)(2,1)} %own_hi.15, bf16[1024,3584]{1,0:T(8,128)(2,1)} %own_hi.15, ...), custom_call_target="tpu_custom_call" | custom-call | flops 4294967296 | bytes 12582912 | tf_op jit(solution)/shard_map/products/pallas_call | solution.py:74
  99.9 10.0 %products.15 = (bf16[3,512,512]{2,1,0:T(8,128)(2,1)}, f32[512,512]{1,0:T(8,128)}) custom-call(s32[4]{0:T(128)} %compare_select_fusion.1.table, bf16[4,512,1024]{2,1,0:T(8,128)(2,1)} %turn.2.own_go, bf16[4,512,1024]{2,1,0:T(8,128)(2,1)} %collective-permute-done.peer_go, bf16[1024,3584]{1,0:T(8,128)(2,1)} %own_hi.15, bf16[1024,3584]{1,0:T(8,128)(2,1)} %own_hi.15, ...), custom_call_target="tpu_custom_call" | custom-call | flops 4294967296 | bytes 12582912 | tf_op jit(solution)/shard_map/products/pallas_call | solution.py:74
  116.2 17.7 %collective-permute-done.11.refs_0_ = bf16[3,512,512]{2,1,0:T(8,128)(2,1)S(1)} collective-permute-done((bf16[3,512,512]{2,1,0:T(8,128)(2,1)}, bf16[3,512,512]{2,1,0:T(8,128)(2,1)S(1)}, u32[]{:S(2)}, u32[]{:S(2)}) %collective-permute-start.11) | collective-permute-done | bytes 1572896 | tf_op jit(solution)/shard_map/ppermute | solution.py:263
  134.9 32.7 %collective-permute-done.17.refs_0_ = bf16[3,512,512]{2,1,0:T(8,128)(2,1)} collective-permute-done((bf16[3,512,512]{2,1,0:T(8,128)(2,1)}, bf16[3,512,512]{2,1,0:T(8,128)(2,1)}, u32[]{:S(2)}, u32[]{:S(2)}) %collective-permute-start.17) | collective-permute-done | bytes 1572896 | tf_op jit(solution)/shard_map/ppermute | solution.py:263
  169.8 31.4 %collective-permute-done.20.refs_0_ = bf16[3,512,512]{2,1,0:T(8,128)(2,1)} collective-permute-done((bf16[3,512,512]{2,1,0:T(8,128)(2,1)}, bf16[3,512,512]{2,1,0:T(8,128)(2,1)}, u32[]{:S(2)}, u32[]{:S(2)}) %collective-permute-start.20) | collective-permute-done | bytes 1572896 | tf_op jit(solution)/shard_map/ppermute | solution.py:263
  203.5 31.4 %collective-permute-done.23.refs_0_ = bf16[3,512,512]{2,1,0:T(8,128)(2,1)S(1)} collective-permute-done((bf16[3,512,512]{2,1,0:T(8,128)(2,1)}, bf16[3,512,512]{2,1,0:T(8,128)(2,1)S(1)}, u32[]{:S(2)}, u32[]{:S(2)}) %collective-permute-start.23) | collective-permute-done | bytes 1572896 | tf_op jit(solution)/shard_map/ppermute | solution.py:263
  236.0 31.8 %collective-permute-done.14.refs_0_ = bf16[3,512,512]{2,1,0:T(8,128)(2,1)S(1)} collective-permute-done((bf16[3,512,512]{2,1,0:T(8,128)(2,1)}, bf16[3,512,512]{2,1,0:T(8,128)(2,1)S(1)}, u32[]{:S(2)}, u32[]{:S(2)}) %collective-permute-start.14) | collective-permute-done | bytes 1572896 | tf_op jit(solution)/shard_map/ppermute | solution.py:263
  281.2 14.9 %collective-permute-done.19.refs_2_ = bf16[1,512,512]{2,1,0:T(8,128)(2,1)S(1)} collective-permute-done((bf16[1,512,512]{2,1,0:T(8,128)(2,1)S(1)}, bf16[1,512,512]{2,1,0:T(8,128)(2,1)S(1)}, u32[]{:S(2)}, u32[]{:S(2)}) %collective-permute-start.19) | collective-permute-done | bytes 524320 | tf_op jit(solution)/shard_map/ppermute | solution.py:263
  299.1 9.2 %collective-permute-done.22.refs_2_ = bf16[1,512,512]{2,1,0:T(8,128)(2,1)S(1)} collective-permute-done((bf16[1,512,512]{2,1,0:T(8,128)(2,1)S(1)}, bf16[1,512,512]{2,1,0:T(8,128)(2,1)S(1)}, u32[]{:S(2)}, u32[]{:S(2)}) %collective-permute-start.22) | collective-permute-done | bytes 524320 | tf_op jit(solution)/shard_map/ppermute | solution.py:263
  311.4 19.5 %collective-permute-done.25.refs_2_ = bf16[1,512,512]{2,1,0:T(8,128)(2,1)S(1)} collective-permute-done((bf16[1,512,512]{2,1,0:T(8,128)(2,1)S(1)}, bf16[1,512,512]{2,1,0:T(8,128)(2,1)S(1)}, u32[]{:S(2)}, u32[]{:S(2)}) %collective-permute-start.25) | collective-permute-done | bytes 524320 | tf_op jit(solution)/shard_map/ppermute | solution.py:263
  332.9 5.8 adam.8
  338.8 5.8 adam.9
  344.6 5.8 adam.10
  350.5 16.7 %collective-permute-done.16.refs_2_ = bf16[1,512,512]{2,1,0:T(8,128)(2,1)} collective-permute-done((bf16[1,512,512]{2,1,0:T(8,128)(2,1)}, bf16[1,512,512]{2,1,0:T(8,128)(2,1)}, u32[]{:S(2)}, u32[]{:S(2)}) %collective-permute-start.16) | collective-permute-done | bytes 524320 | tf_op jit(solution)/shard_map/ppermute | solution.py:263
  367.1 5.8 adam.11
  373.8 5.7 adam.12
  380.3 5.7 adam.13
  386.1 4.5 adam.14
  391.4 4.7 adam.15
  398.6 3.6 collective-permute-start.32
  406.3 34.7 %collective-permute-done.32 = bf16[528,128]{1,0:T(8,128)(2,1)S(1)} collective-permute-done((bf16[528,128]{1,0:T(8,128)(2,1)S(1)}, bf16[528,128]{1,0:T(8,128)(2,1)S(1)}, u32[]{:S(2)}, u32[]{:S(2)}) %collective-permute-start.32) | collective-permute-done | bytes 135200 | tf_op jit(solution)/shard_map/ppermute | solution.py:263
  441.0 21.2 %collective-permute-start.31 = (bf16[528,128]{1,0:T(8,128)(2,1)S(1)}, bf16[528,128]{1,0:T(8,128)(2,1)S(1)}, u32[]{:S(2)}, u32[]{:S(2)}) collective-permute-start(bf16[528,128]{1,0:T(8,128)(2,1)S(1)} %copy-done.59), channel_id=1, source_target_pairs={{0,2},{1,10},{2,18},{3,26},{4,6},{5,14},{6,22},{7,30},{8,3},{9,11}... | collective-permute-start | bytes 405512 | tf_op jit(solution)/shard_map/ppermute | solution.py:263
  462.2 12.4 %collective-permute-done.31 = bf16[528,128]{1,0:T(8,128)(2,1)S(1)} collective-permute-done((bf16[528,128]{1,0:T(8,128)(2,1)S(1)}, bf16[528,128]{1,0:T(8,128)(2,1)S(1)}, u32[]{:S(2)}, u32[]{:S(2)}) %collective-permute-start.31) | collective-permute-done | bytes 135200 | tf_op jit(solution)/shard_map/ppermute | solution.py:263
  474.6 43.5 %collective-permute-start.47 = (bf16[528,256]{1,0:T(8,128)(2,1)S(1)}, bf16[528,256]{1,0:T(8,128)(2,1)S(1)}, u32[]{:S(2)}, u32[]{:S(2)}) collective-permute-start(bf16[528,256]{1,0:T(8,128)(2,1)S(1)} %copy-done.56), channel_id=1, source_target_pairs={{0,7},{1,15},{2,23},{3,31},{4,3},{5,11},{6,19},{7,27},{8,6},{9,14}... | collective-permute-start | bytes 811016 | tf_op jit(solution)/shard_map/ppermute | solution.py:263
  521.4 4.2 collective-permute-done.47
  525.7 7.1 collective-permute-done.46
  532.9 22.4 %collective-permute-done.52 = bf16[528,256]{1,0:T(8,128)(2,1)S(1)} collective-permute-done((bf16[528,256]{1,0:T(8,128)(2,1)S(1)}, bf16[528,256]{1,0:T(8,128)(2,1)S(1)}, u32[]{:S(2)}, u32[]{:S(2)}) %collective-permute-start.52) | collective-permute-done | bytes 270368 | tf_op jit(solution)/shard_map/ppermute | solution.py:263
  555.2 25.1 %collective-permute-start.38 = (bf16[2,528,256]{2,1,0:T(8,128)(2,1)S(1)}, bf16[2,528,256]{2,1,0:T(8,128)(2,1)S(1)}, u32[]{:S(2)}, u32[]{:S(2)}) collective-permute-start(bf16[2,528,256]{2,1,0:T(8,128)(2,1)S(1)} %pad_maximum_fusion.refs_0_), channel_id=1, source_target_pairs={{0,1},{1,0},{2,3},{3,2},{4,5},{5,4},{6,7},{7,6},{8,9},{9,8},{10,11... | collective-permute-start | bytes 1622024 | tf_op jit(solution)/shard_map/ppermute | solution.py:263
  580.3 22.5 %collective-permute-start.39 = (bf16[2,528,256]{2,1,0:T(8,128)(2,1)S(1)}, bf16[2,528,256]{2,1,0:T(8,128)(2,1)S(1)}, u32[]{:S(2)}, u32[]{:S(2)}) collective-permute-start(bf16[2,528,256]{2,1,0:T(8,128)(2,1)S(1)} %pad_maximum_fusion.refs_0_), channel_id=1, source_target_pairs={{0,2},{1,3},{2,0},{3,1},{4,6},{5,7},{6,4},{7,5},{8,10},{9,11},{10,... | collective-permute-start | bytes 1622024 | tf_op jit(solution)/shard_map/ppermute | solution.py:263
  602.8 11.5 %collective-permute-done.57 = bf16[528,256]{1,0:T(8,128)(2,1)S(1)} collective-permute-done((bf16[528,256]{1,0:T(8,128)(2,1)S(1)}, bf16[528,256]{1,0:T(8,128)(2,1)S(1)}, u32[]{:S(2)}, u32[]{:S(2)}) %collective-permute-start.57) | collective-permute-done | bytes 270368 | tf_op jit(solution)/shard_map/ppermute | solution.py:263
  614.4 18.9 %collective-permute-done.56 = bf16[528,256]{1,0:T(8,128)(2,1)S(1)} collective-permute-done((bf16[528,256]{1,0:T(8,128)(2,1)S(1)}, bf16[528,256]{1,0:T(8,128)(2,1)S(1)}, u32[]{:S(2)}, u32[]{:S(2)}) %collective-permute-start.56) | collective-permute-done | bytes 270368 | tf_op jit(solution)/shard_map/ppermute | solution.py:263
  634.2 4.9 collective-permute-start.33
  639.2 6.4 collective-permute-start.43
  645.7 3.9 collective-permute-done.33.refs_1_
  649.6 3.9 collective-permute-start.45
  654.4 6.8 collective-permute-done.43.refs_1_
  661.2 14.7 %collective-permute-done.44.refs_2_ = bf16[2,528,256]{2,1,0:T(8,128)(2,1)S(1)} collective-permute-done((bf16[2,528,256]{2,1,0:T(8,128)(2,1)S(1)}, bf16[2,528,256]{2,1,0:T(8,128)(2,1)S(1)}, u32[]{:S(2)}, u32[]{:S(2)}) %collective-permute-start.44) | collective-permute-done | bytes 540704 | tf_op jit(solution)/shard_map/ppermute | solution.py:263
  678.4 6.0 collective-permute-done.48.refs_1_
  684.4 14.7 %collective-permute-done.49.refs_2_ = bf16[2,528,256]{2,1,0:T(8,128)(2,1)S(1)} collective-permute-done((bf16[2,528,256]{2,1,0:T(8,128)(2,1)S(1)}, bf16[2,528,256]{2,1,0:T(8,128)(2,1)S(1)}, u32[]{:S(2)}, u32[]{:S(2)}) %collective-permute-start.49) | collective-permute-done | bytes 540704 | tf_op jit(solution)/shard_map/ppermute | solution.py:263
  701.7 5.9 collective-permute-done.53.refs_1_
  707.6 14.6 %collective-permute-done.54.refs_2_ = bf16[2,528,256]{2,1,0:T(8,128)(2,1)S(1)} collective-permute-done((bf16[2,528,256]{2,1,0:T(8,128)(2,1)S(1)}, bf16[2,528,256]{2,1,0:T(8,128)(2,1)S(1)}, u32[]{:S(2)}, u32[]{:S(2)}) %collective-permute-start.54) | collective-permute-done | bytes 540704 | tf_op jit(solution)/shard_map/ppermute | solution.py:263
  724.7 6.1 collective-permute-done.58.refs_1_
  733.3 12.2 %collective-permute-done.59.refs_2_ = bf16[2,528,256]{2,1,0:T(8,128)(2,1)} collective-permute-done((bf16[2,528,256]{2,1,0:T(8,128)(2,1)S(1)}, bf16[2,528,256]{2,1,0:T(8,128)(2,1)}, u32[]{:S(2)}, u32[]{:S(2)}) %collective-permute-start.59) | collective-permute-done | bytes 540704 | tf_op jit(solution)/shard_map/ppermute | solution.py:263
  748.0 6.0 collective-permute-done.63.refs_1_
  754.0 20.4 %collective-permute-done.64.refs_2_ = bf16[2,528,256]{2,1,0:T(8,128)(2,1)} collective-permute-done((bf16[2,528,256]{2,1,0:T(8,128)(2,1)S(1)}, bf16[2,528,256]{2,1,0:T(8,128)(2,1)}, u32[]{:S(2)}, u32[]{:S(2)}) %collective-permute-start.64) | collective-permute-done | bytes 540704 | tf_op jit(solution)/shard_map/ppermute | solution.py:263
  774.5 3.9 collective-permute-start.35
  780.1 4.1 place.8
  784.3 4.1 place.9
  788.4 4.1 place.10
  792.6 4.1 place.11
  796.7 4.1 place.12
  800.8 4.1 place.13
  804.9 3.5 place.14
  808.5 3.5 place.15
  (250 shorter events, 76.2 us)
Async XLA Ops:
  0.6 18.2 %collective-permute-start.1 = (bf16[1024,3584]{1,0:T(8,128)(2,1)}, bf16[1024,3584]{1,0:T(8,128)(2,1)}, u32[]{:S(2)}, u32[]{:S(2)}) collective-permute-start(bf16[1024,3584]{1,0:T(8,128)(2,1)} %own_hi.15), channel_id=1, source_target_pairs={{0,4},{1,5},{2,6},{3,7},{4,0},{5,1},{6,2},{7,3},{8,12},{9,13},{10,... | collective-permute-start | bytes 22020104 | tf_op jit(solution)/shard_map/ppermute | solution.py:263
  7.6 11.2 %collective-permute-start = (bf16[4,512,1024]{2,1,0:T(8,128)(2,1)}, bf16[4,512,1024]{2,1,0:T(8,128)(2,1)}, u32[]{:S(2)}, u32[]{:S(2)}) collective-permute-start(bf16[4,512,1024]{2,1,0:T(8,128)(2,1)} %turn.3), channel_id=1, source_target_pairs={{0,4},{1,5},{2,6},{3,7},{4,0},{5,1},{6,2},{7,3},{8,12},{9,13},{10,... | collective-permute-start | bytes 12582920 | tf_op jit(solution)/shard_map/ppermute | solution.py:263
  26.5 71.0 %collective-permute-start.2 = (bf16[3,512,256]{2,1,0:T(8,128)(2,1)}, bf16[3,512,256]{2,1,0:T(8,128)(2,1)}, u32[]{:S(2)}, u32[]{:S(2)}) collective-permute-start(bf16[3,512,256]{2,1,0:T(8,128)(2,1)} %get-tuple-element.78), channel_id=1, source_target_pairs={{0,8},{1,9},{2,10},{3,11},{4,12},{5,13},{6,14},{7,15},{24,16},{25,... | collective-permute-start | bytes 2359304 | tf_op jit(solution)/shard_map/ppermute | solution.py:263
  40.0 69.9 %collective-permute-start.5 = (bf16[3,512,256]{2,1,0:T(8,128)(2,1)}, bf16[3,512,256]{2,1,0:T(8,128)(2,1)}, u32[]{:S(2)}, u32[]{:S(2)}) collective-permute-start(bf16[3,512,256]{2,1,0:T(8,128)(2,1)} %get-tuple-element.80), channel_id=1, source_target_pairs={{0,8},{1,9},{2,10},{3,11},{4,12},{5,13},{6,14},{7,15},{24,16},{25,... | collective-permute-start | bytes 2359304 | tf_op jit(solution)/shard_map/ppermute | solution.py:263
  52.1 60.7 %collective-permute-start.8 = (bf16[3,512,512]{2,1,0:T(8,128)(2,1)}, bf16[3,512,512]{2,1,0:T(8,128)(2,1)S(1)}, u32[]{:S(2)}, u32[]{:S(2)}) collective-permute-start(bf16[3,512,512]{2,1,0:T(8,128)(2,1)} %get-tuple-element.82), channel_id=1, source_target_pairs={{0,8},{1,9},{2,10},{3,11},{4,12},{5,13},{6,14},{7,15},{24,16},{25,... | collective-permute-start | bytes 4718600 | tf_op jit(solution)/shard_map/ppermute | solution.py:263
  63.6 70.3 %collective-permute-start.11 = (bf16[3,512,512]{2,1,0:T(8,128)(2,1)}, bf16[3,512,512]{2,1,0:T(8,128)(2,1)S(1)}, u32[]{:S(2)}, u32[]{:S(2)}) collective-permute-start(bf16[3,512,512]{2,1,0:T(8,128)(2,1)} %get-tuple-element.84), channel_id=1, source_target_pairs={{0,8},{1,9},{2,10},{3,11},{4,12},{5,13},{6,14},{7,15},{24,16},{25,... | collective-permute-start | bytes 4718600 | tf_op jit(solution)/shard_map/ppermute | solution.py:263
  75.0 92.6 %collective-permute-start.17 = (bf16[3,512,512]{2,1,0:T(8,128)(2,1)}, bf16[3,512,512]{2,1,0:T(8,128)(2,1)}, u32[]{:S(2)}, u32[]{:S(2)}) collective-permute-start(bf16[3,512,512]{2,1,0:T(8,128)(2,1)} %get-tuple-element.88), channel_id=1, source_target_pairs={{0,8},{1,9},{2,10},{3,11},{4,12},{5,13},{6,14},{7,15},{24,16},{25,... | collective-permute-start | bytes 4718600 | tf_op jit(solution)/shard_map/ppermute | solution.py:263
  97.5 103.8 %collective-permute-start.20 = (bf16[3,512,512]{2,1,0:T(8,128)(2,1)}, bf16[3,512,512]{2,1,0:T(8,128)(2,1)}, u32[]{:S(2)}, u32[]{:S(2)}) collective-permute-start(bf16[3,512,512]{2,1,0:T(8,128)(2,1)} %get-tuple-element.90), channel_id=1, source_target_pairs={{0,8},{1,9},{2,10},{3,11},{4,12},{5,13},{6,14},{7,15},{24,16},{25,... | collective-permute-start | bytes 4718600 | tf_op jit(solution)/shard_map/ppermute | solution.py:263
  109.9 125.0 %collective-permute-start.23 = (bf16[3,512,512]{2,1,0:T(8,128)(2,1)}, bf16[3,512,512]{2,1,0:T(8,128)(2,1)S(1)}, u32[]{:S(2)}, u32[]{:S(2)}) collective-permute-start(bf16[3,512,512]{2,1,0:T(8,128)(2,1)} %get-tuple-element.92), channel_id=1, source_target_pairs={{0,8},{1,9},{2,10},{3,11},{4,12},{5,13},{6,14},{7,15},{24,16},{25,... | collective-permute-start | bytes 4718600 | tf_op jit(solution)/shard_map/ppermute | solution.py:263
  112.8 155.0 %collective-permute-start.14 = (bf16[3,512,512]{2,1,0:T(8,128)(2,1)}, bf16[3,512,512]{2,1,0:T(8,128)(2,1)S(1)}, u32[]{:S(2)}, u32[]{:S(2)}) collective-permute-start(bf16[3,512,512]{2,1,0:T(8,128)(2,1)} %get-tuple-element.86), channel_id=1, source_target_pairs={{0,8},{1,9},{2,10},{3,11},{4,12},{5,13},{6,14},{7,15},{24,16},{25,... | collective-permute-start | bytes 4718600 | tf_op jit(solution)/shard_map/ppermute | solution.py:263
  133.8 135.2 %collective-permute-start.9 = (bf16[2,512,512]{2,1,0:T(8,128)(2,1)S(1)}, bf16[2,512,512]{2,1,0:T(8,128)(2,1)S(1)}, u32[]{:S(2)}, u32[]{:S(2)}) collective-permute-start(bf16[2,512,512]{2,1,0:T(8,128)(2,1)S(1)} %add_convert_fusion.5), channel_id=1, source_target_pairs={{8,16},{9,17},{10,18},{11,19},{12,20},{13,21},{14,22},{15,23},{16,... | collective-permute-start | bytes 3145736 | tf_op jit(solution)/shard_map/ppermute | solution.py:263
  167.5 103.3 %collective-permute-start.12 = (bf16[2,512,512]{2,1,0:T(8,128)(2,1)S(1)}, bf16[2,512,512]{2,1,0:T(8,128)(2,1)S(1)}, u32[]{:S(2)}, u32[]{:S(2)}) collective-permute-start(bf16[2,512,512]{2,1,0:T(8,128)(2,1)S(1)} %add_convert_fusion.4), channel_id=1, source_target_pairs={{8,16},{9,17},{10,18},{11,19},{12,20},{13,21},{14,22},{15,23},{16,... | collective-permute-start | bytes 3145736 | tf_op jit(solution)/shard_map/ppermute | solution.py:263
  201.2 71.3 %collective-permute-start.18 = (bf16[2,512,512]{2,1,0:T(8,128)(2,1)S(1)}, bf16[2,512,512]{2,1,0:T(8,128)(2,1)S(1)}, u32[]{:S(2)}, u32[]{:S(2)}) collective-permute-start(bf16[2,512,512]{2,1,0:T(8,128)(2,1)S(1)} %add_convert_fusion.2), channel_id=1, source_target_pairs={{8,16},{9,17},{10,18},{11,19},{12,20},{13,21},{14,22},{15,23},{16,... | collective-permute-start | bytes 3145736 | tf_op jit(solution)/shard_map/ppermute | solution.py:263
  235.0 38.4 %collective-permute-start.21 = (bf16[2,512,512]{2,1,0:T(8,128)(2,1)S(1)}, bf16[2,512,512]{2,1,0:T(8,128)(2,1)S(1)}, u32[]{:S(2)}, u32[]{:S(2)}) collective-permute-start(bf16[2,512,512]{2,1,0:T(8,128)(2,1)S(1)} %add_convert_fusion.1), channel_id=1, source_target_pairs={{8,16},{9,17},{10,18},{11,19},{12,20},{13,21},{14,22},{15,23},{16,... | collective-permute-start | bytes 3145736 | tf_op jit(solution)/shard_map/ppermute | solution.py:263
  269.1 7.2 collective-permute-start.15
  270.8 7.8 collective-permute-start.3
  272.5 7.4 collective-permute-start.6
  273.4 22.7 %collective-permute-start.19 = (bf16[1,512,512]{2,1,0:T(8,128)(2,1)S(1)}, bf16[1,512,512]{2,1,0:T(8,128)(2,1)S(1)}, u32[]{:S(2)}, u32[]{:S(2)}) collective-permute-start(bf16[1,512,512]{2,1,0:T(8,128)(2,1)S(1)} %add_convert_fusion.8), channel_id=1, source_target_pairs={{8,0},{9,1},{10,2},{11,3},{12,4},{13,5},{14,6},{15,7},{16,24},{17,... | collective-permute-start | bytes 1572872 | tf_op jit(solution)/shard_map/ppermute | solution.py:263
  274.9 33.5 %collective-permute-start.22 = (bf16[1,512,512]{2,1,0:T(8,128)(2,1)S(1)}, bf16[1,512,512]{2,1,0:T(8,128)(2,1)S(1)}, u32[]{:S(2)}, u32[]{:S(2)}) collective-permute-start(bf16[1,512,512]{2,1,0:T(8,128)(2,1)S(1)} %add_convert_fusion.7), channel_id=1, source_target_pairs={{8,0},{9,1},{10,2},{11,3},{12,4},{13,5},{14,6},{15,7},{16,24},{17,... | collective-permute-start | bytes 1572872 | tf_op jit(solution)/shard_map/ppermute | solution.py:263
  276.3 54.5 %collective-permute-start.25 = (bf16[1,512,512]{2,1,0:T(8,128)(2,1)S(1)}, bf16[1,512,512]{2,1,0:T(8,128)(2,1)S(1)}, u32[]{:S(2)}, u32[]{:S(2)}) collective-permute-start(bf16[1,512,512]{2,1,0:T(8,128)(2,1)S(1)} %add_convert_fusion.6), channel_id=1, source_target_pairs={{8,0},{9,1},{10,2},{11,3},{12,4},{13,5},{14,6},{15,7},{16,24},{17,... | collective-permute-start | bytes 1572872 | tf_op jit(solution)/shard_map/ppermute | solution.py:263
  278.6 100.9 %collective-permute-start.10 = (bf16[1,512,512]{2,1,0:T(8,128)(2,1)}, bf16[1,512,512]{2,1,0:T(8,128)(2,1)S(1)}, u32[]{:S(2)}, u32[]{:S(2)}) collective-permute-start(bf16[1,512,512]{2,1,0:T(8,128)(2,1)} %add_convert_fusion.11), channel_id=1, source_target_pairs={{8,0},{9,1},{10,2},{11,3},{12,4},{13,5},{14,6},{15,7},{16,24},{17,... | collective-permute-start | bytes 1572872 | tf_op jit(solution)/shard_map/ppermute | solution.py:263
  279.9 93.0 %collective-permute-start.13 = (bf16[1,512,512]{2,1,0:T(8,128)(2,1)}, bf16[1,512,512]{2,1,0:T(8,128)(2,1)S(1)}, u32[]{:S(2)}, u32[]{:S(2)}) collective-permute-start(bf16[1,512,512]{2,1,0:T(8,128)(2,1)} %add_convert_fusion.10), channel_id=1, source_target_pairs={{8,0},{9,1},{10,2},{11,3},{12,4},{13,5},{14,6},{15,7},{16,24},{17,... | collective-permute-start | bytes 1572872 | tf_op jit(solution)/shard_map/ppermute | solution.py:263
  296.1 71.0 %collective-permute-start.16 = (bf16[1,512,512]{2,1,0:T(8,128)(2,1)}, bf16[1,512,512]{2,1,0:T(8,128)(2,1)}, u32[]{:S(2)}, u32[]{:S(2)}) collective-permute-start(bf16[1,512,512]{2,1,0:T(8,128)(2,1)} %add_convert_fusion.9), channel_id=1, source_target_pairs={{8,0},{9,1},{10,2},{11,3},{12,4},{13,5},{14,6},{15,7},{16,24},{17,... | collective-permute-start | bytes 1572872 | tf_op jit(solution)/shard_map/ppermute | solution.py:263
  308.4 77.7 %collective-permute-start.7 = (bf16[1,512,256]{2,1,0:T(8,128)(2,1)}, bf16[1,512,256]{2,1,0:T(8,128)(2,1)}, u32[]{:S(2)}, u32[]{:S(2)}) collective-permute-start(bf16[1,512,256]{2,1,0:T(8,128)(2,1)} %add_convert_fusion.14), channel_id=1, source_target_pairs={{8,0},{9,1},{10,2},{11,3},{12,4},{13,5},{14,6},{15,7},{16,24},{17,... | collective-permute-start | bytes 786440 | tf_op jit(solution)/shard_map/ppermute | solution.py:263
  331.6 59.0 %collective-permute-start.4 = (bf16[1,512,256]{2,1,0:T(8,128)(2,1)}, bf16[1,512,256]{2,1,0:T(8,128)(2,1)S(1)}, u32[]{:S(2)}, u32[]{:S(2)}) collective-permute-start(bf16[1,512,256]{2,1,0:T(8,128)(2,1)} %add_convert_fusion.15), channel_id=1, source_target_pairs={{8,0},{9,1},{10,2},{11,3},{12,4},{13,5},{14,6},{15,7},{16,24},{17,... | collective-permute-start | bytes 786440 | tf_op jit(solution)/shard_map/ppermute | solution.py:263
  396.1 8.1 collective-permute-start.27
  396.1 9.4 %collective-permute-start.26 = (bf16[528,128]{1,0:T(8,128)(2,1)}, bf16[528,128]{1,0:T(8,128)(2,1)S(1)}, u32[]{:S(2)}, u32[]{:S(2)}) collective-permute-start(bf16[528,128]{1,0:T(8,128)(2,1)} %get-tuple-element.117), channel_id=1, source_target_pairs={{0,3},{1,11},{2,19},{3,27},{4,7},{5,15},{6,23},{7,31},{8,2},{9,10}... | collective-permute-start | bytes 405512 | tf_op jit(solution)/shard_map/ppermute | solution.py:263
  398.6 42.3 %collective-permute-start.32 = (bf16[528,128]{1,0:T(8,128)(2,1)S(1)}, bf16[528,128]{1,0:T(8,128)(2,1)S(1)}, u32[]{:S(2)}, u32[]{:S(2)}) collective-permute-start(bf16[528,128]{1,0:T(8,128)(2,1)S(1)} %copy-done.60), channel_id=1, source_target_pairs={{0,6},{1,14},{2,22},{3,30},{4,2},{5,10},{6,18},{7,26},{8,7},{9,15}... | collective-permute-start | bytes 405512 | tf_op jit(solution)/shard_map/ppermute | solution.py:263
  402.3 115.8 %collective-permute-start.37 = (bf16[528,256]{1,0:T(8,128)(2,1)}, bf16[528,256]{1,0:T(8,128)(2,1)S(1)}, u32[]{:S(2)}, u32[]{:S(2)}) collective-permute-start(bf16[528,256]{1,0:T(8,128)(2,1)} %get-tuple-element.122), channel_id=1, source_target_pairs={{0,5},{1,13},{2,21},{3,29},{4,1},{5,9},{6,17},{7,25},{8,4},{9,12},... | collective-permute-start | bytes 811016 | tf_op jit(solution)/shard_map/ppermute | solution.py:263
  402.9 115.7 %collective-permute-start.36 = (bf16[528,256]{1,0:T(8,128)(2,1)}, bf16[528,256]{1,0:T(8,128)(2,1)S(1)}, u32[]{:S(2)}, u32[]{:S(2)}) collective-permute-start(bf16[528,256]{1,0:T(8,128)(2,1)} %get-tuple-element.121), channel_id=1, source_target_pairs={{0,1},{1,9},{2,17},{3,25},{4,5},{5,13},{6,21},{7,29},{8,0},{9,8},{... | collective-permute-start | bytes 811016 | tf_op jit(solution)/shard_map/ppermute | solution.py:263
  404.2 114.4 %collective-permute-start.42 = (bf16[528,256]{1,0:T(8,128)(2,1)S(1)}, bf16[528,256]{1,0:T(8,128)(2,1)S(1)}, u32[]{:S(2)}, u32[]{:S(2)}) collective-permute-start(bf16[528,256]{1,0:T(8,128)(2,1)S(1)} %copy-done.58), channel_id=1, source_target_pairs={{0,4},{1,12},{2,20},{3,28},{4,0},{5,8},{6,16},{7,24},{8,5},{9,13},... | collective-permute-start | bytes 811016 | tf_op jit(solution)/shard_map/ppermute | solution.py:263
  405.6 113.1 %collective-permute-start.41 = (bf16[528,256]{1,0:T(8,128)(2,1)S(1)}, bf16[528,256]{1,0:T(8,128)(2,1)S(1)}, u32[]{:S(2)}, u32[]{:S(2)}) collective-permute-start(bf16[528,256]{1,0:T(8,128)(2,1)S(1)} %copy-done.57), channel_id=1, source_target_pairs={{0,0},{1,8},{2,16},{3,24},{4,4},{5,12},{6,20},{7,28},{8,1},{9,9},{... | collective-permute-start | bytes 811016 | tf_op jit(solution)/shard_map/ppermute | solution.py:263
  441.0 33.6 %collective-permute-start.31 = (bf16[528,128]{1,0:T(8,128)(2,1)S(1)}, bf16[528,128]{1,0:T(8,128)(2,1)S(1)}, u32[]{:S(2)}, u32[]{:S(2)}) collective-permute-start(bf16[528,128]{1,0:T(8,128)(2,1)S(1)} %copy-done.59), channel_id=1, source_target_pairs={{0,2},{1,10},{2,18},{3,26},{4,6},{5,14},{6,22},{7,30},{8,3},{9,11}... | collective-permute-start | bytes 405512 | tf_op jit(solution)/shard_map/ppermute | solution.py:263
  474.6 51.1 %collective-permute-start.47 = (bf16[528,256]{1,0:T(8,128)(2,1)S(1)}, bf16[528,256]{1,0:T(8,128)(2,1)S(1)}, u32[]{:S(2)}, u32[]{:S(2)}) collective-permute-start(bf16[528,256]{1,0:T(8,128)(2,1)S(1)} %copy-done.56), channel_id=1, source_target_pairs={{0,7},{1,15},{2,23},{3,31},{4,3},{5,11},{6,19},{7,27},{8,6},{9,14}... | collective-permute-start | bytes 811016 | tf_op jit(solution)/shard_map/ppermute | solution.py:263
  518.0 14.7 %collective-permute-start.46 = (bf16[528,256]{1,0:T(8,128)(2,1)S(1)}, bf16[528,256]{1,0:T(8,128)(2,1)S(1)}, u32[]{:S(2)}, u32[]{:S(2)}) collective-permute-start(bf16[528,256]{1,0:T(8,128)(2,1)S(1)} %copy-done.55), channel_id=1, source_target_pairs={{0,3},{1,11},{2,19},{3,27},{4,7},{5,15},{6,23},{7,31},{8,2},{9,10}... | collective-permute-start | bytes 811016 | tf_op jit(solution)/shard_map/ppermute | solution.py:263
  518.6 36.6 %collective-permute-start.52 = (bf16[528,256]{1,0:T(8,128)(2,1)S(1)}, bf16[528,256]{1,0:T(8,128)(2,1)S(1)}, u32[]{:S(2)}, u32[]{:S(2)}) collective-permute-start(bf16[528,256]{1,0:T(8,128)(2,1)S(1)} %copy-done.54), channel_id=1, source_target_pairs={{0,6},{1,14},{2,22},{3,30},{4,2},{5,10},{6,18},{7,26},{8,7},{9,15}... | collective-permute-start | bytes 811016 | tf_op jit(solution)/shard_map/ppermute | solution.py:263
  518.6 61.7 %collective-permute-start.51 = (bf16[528,256]{1,0:T(8,128)(2,1)S(1)}, bf16[528,256]{1,0:T(8,128)(2,1)S(1)}, u32[]{:S(2)}, u32[]{:S(2)}) collective-permute-start(bf16[528,256]{1,0:T(8,128)(2,1)S(1)} %copy-done.53), channel_id=1, source_target_pairs={{0,2},{1,10},{2,18},{3,26},{4,6},{5,14},{6,22},{7,30},{8,3},{9,11}... | collective-permute-start | bytes 811016 | tf_op jit(solution)/shard_map/ppermute | solution.py:263
  518.7 95.6 %collective-permute-start.57 = (bf16[528,256]{1,0:T(8,128)(2,1)S(1)}, bf16[528,256]{1,0:T(8,128)(2,1)S(1)}, u32[]{:S(2)}, u32[]{:S(2)}) collective-permute-start(bf16[528,256]{1,0:T(8,128)(2,1)S(1)} %copy-done.52), channel_id=1, source_target_pairs={{0,5},{1,13},{2,21},{3,29},{4,1},{5,9},{6,17},{7,25},{8,4},{9,12},... | collective-permute-start | bytes 811016 | tf_op jit(solution)/shard_map/ppermute | solution.py:263
  525.7 107.6 %collective-permute-start.56 = (bf16[528,256]{1,0:T(8,128)(2,1)S(1)}, bf16[528,256]{1,0:T(8,128)(2,1)S(1)}, u32[]{:S(2)}, u32[]{:S(2)}) collective-permute-start(bf16[528,256]{1,0:T(8,128)(2,1)S(1)} %copy-done.51), channel_id=1, source_target_pairs={{0,1},{1,9},{2,17},{3,25},{4,5},{5,13},{6,21},{7,29},{8,0},{9,8},{... | collective-permute-start | bytes 811016 | tf_op jit(solution)/shard_map/ppermute | solution.py:263
  532.8 101.4 %collective-permute-start.62 = (bf16[528,256]{1,0:T(8,128)(2,1)S(1)}, bf16[528,256]{1,0:T(8,128)(2,1)S(1)}, u32[]{:S(2)}, u32[]{:S(2)}) collective-permute-start(bf16[528,256]{1,0:T(8,128)(2,1)S(1)} %copy-done.50), channel_id=1, source_target_pairs={{0,4},{1,12},{2,20},{3,28},{4,0},{5,8},{6,16},{7,24},{8,5},{9,13},... | collective-permute-start | bytes 811016 | tf_op jit(solution)/shard_map/ppermute | solution.py:263
  555.2 94.4 %collective-permute-start.38 = (bf16[2,528,256]{2,1,0:T(8,128)(2,1)S(1)}, bf16[2,528,256]{2,1,0:T(8,128)(2,1)S(1)}, u32[]{:S(2)}, u32[]{:S(2)}) collective-permute-start(bf16[2,528,256]{2,1,0:T(8,128)(2,1)S(1)} %pad_maximum_fusion.refs_0_), channel_id=1, source_target_pairs={{0,1},{1,0},{2,3},{3,2},{4,5},{5,4},{6,7},{7,6},{8,9},{9,8},{10,11... | collective-permute-start | bytes 1622024 | tf_op jit(solution)/shard_map/ppermute | solution.py:263
  580.3 73.2 %collective-permute-start.39 = (bf16[2,528,256]{2,1,0:T(8,128)(2,1)S(1)}, bf16[2,528,256]{2,1,0:T(8,128)(2,1)S(1)}, u32[]{:S(2)}, u32[]{:S(2)}) collective-permute-start(bf16[2,528,256]{2,1,0:T(8,128)(2,1)S(1)} %pad_maximum_fusion.refs_0_), channel_id=1, source_target_pairs={{0,2},{1,3},{2,0},{3,1},{4,6},{5,7},{6,4},{7,5},{8,10},{9,11},{10,... | collective-permute-start | bytes 1622024 | tf_op jit(solution)/shard_map/ppermute | solution.py:263
  614.3 39.2 %collective-permute-start.40 = (bf16[2,528,256]{2,1,0:T(8,128)(2,1)S(1)}, bf16[2,528,256]{2,1,0:T(8,128)(2,1)S(1)}, u32[]{:S(2)}, u32[]{:S(2)}) collective-permute-start(bf16[2,528,256]{2,1,0:T(8,128)(2,1)S(1)} %pad_maximum_fusion.refs_0_), channel_id=1, source_target_pairs={{0,3},{1,2},{2,1},{3,0},{4,7},{5,6},{6,5},{7,4},{8,11},{9,10},{10,... | collective-permute-start | bytes 1622024 | tf_op jit(solution)/shard_map/ppermute | solution.py:263
  634.2 15.4 %collective-permute-start.33 = (bf16[2,528,128]{2,1,0:T(8,128)(2,1)S(1)}, bf16[2,528,128]{2,1,0:T(8,128)(2,1)S(1)}, u32[]{:S(2)}, u32[]{:S(2)}) collective-permute-start(bf16[2,528,128]{2,1,0:T(8,128)(2,1)S(1)} %pad_maximum_fusion.7.refs_0_), channel_id=1, source_target_pairs={{0,1},{1,0},{2,3},{3,2},{4,5},{5,4},{6,7},{7,6},{8,9},{9,8},{10,11... | collective-permute-start | bytes 811016 | tf_op jit(solution)/shard_map/ppermute | solution.py:263
  639.2 21.9 %collective-permute-start.43 = (bf16[2,528,256]{2,1,0:T(8,128)(2,1)S(1)}, bf16[2,528,256]{2,1,0:T(8,128)(2,1)S(1)}, u32[]{:S(2)}, u32[]{:S(2)}) collective-permute-start(bf16[2,528,256]{2,1,0:T(8,128)(2,1)S(1)} %pad_maximum_fusion.1.refs_0_), channel_id=1, source_target_pairs={{0,1},{1,0},{2,3},{3,2},{4,5},{5,4},{6,7},{7,6},{8,9},{9,8},{10,11... | collective-permute-start | bytes 1622024 | tf_op jit(solution)/shard_map/ppermute | solution.py:263
  649.6 26.3 %collective-permute-start.44 = (bf16[2,528,256]{2,1,0:T(8,128)(2,1)S(1)}, bf16[2,528,256]{2,1,0:T(8,128)(2,1)S(1)}, u32[]{:S(2)}, u32[]{:S(2)}) collective-permute-start(bf16[2,528,256]{2,1,0:T(8,128)(2,1)S(1)} %pad_maximum_fusion.1.refs_0_), channel_id=1, source_target_pairs={{0,2},{1,3},{2,0},{3,1},{4,6},{5,7},{6,4},{7,5},{8,10},{9,11},{10,... | collective-permute-start | bytes 1622024 | tf_op jit(solution)/shard_map/ppermute | solution.py:263
  649.6 28.8 %collective-permute-start.45 = (bf16[2,528,256]{2,1,0:T(8,128)(2,1)S(1)}, bf16[2,528,256]{2,1,0:T(8,128)(2,1)S(1)}, u32[]{:S(2)}, u32[]{:S(2)}) collective-permute-start(bf16[2,528,256]{2,1,0:T(8,128)(2,1)S(1)} %pad_maximum_fusion.1.refs_0_), channel_id=1, source_target_pairs={{0,3},{1,2},{2,1},{3,0},{4,7},{5,6},{6,5},{7,4},{8,11},{9,10},{10,... | collective-permute-start | bytes 1622024 | tf_op jit(solution)/shard_map/ppermute | solution.py:263
  653.5 30.9 %collective-permute-start.48 = (bf16[2,528,256]{2,1,0:T(8,128)(2,1)S(1)}, bf16[2,528,256]{2,1,0:T(8,128)(2,1)S(1)}, u32[]{:S(2)}, u32[]{:S(2)}) collective-permute-start(bf16[2,528,256]{2,1,0:T(8,128)(2,1)S(1)} %pad_maximum_fusion.2.refs_0_), channel_id=1, source_target_pairs={{0,1},{1,0},{2,3},{3,2},{4,5},{5,4},{6,7},{7,6},{8,9},{9,8},{10,11... | collective-permute-start | bytes 1622024 | tf_op jit(solution)/shard_map/ppermute | solution.py:263
  653.6 45.5 %collective-permute-start.49 = (bf16[2,528,256]{2,1,0:T(8,128)(2,1)S(1)}, bf16[2,528,256]{2,1,0:T(8,128)(2,1)S(1)}, u32[]{:S(2)}, u32[]{:S(2)}) collective-permute-start(bf16[2,528,256]{2,1,0:T(8,128)(2,1)S(1)} %pad_maximum_fusion.2.refs_0_), channel_id=1, source_target_pairs={{0,2},{1,3},{2,0},{3,1},{4,6},{5,7},{6,4},{7,5},{8,10},{9,11},{10,... | collective-permute-start | bytes 1622024 | tf_op jit(solution)/shard_map/ppermute | solution.py:263
  661.2 40.5 %collective-permute-start.50 = (bf16[2,528,256]{2,1,0:T(8,128)(2,1)S(1)}, bf16[2,528,256]{2,1,0:T(8,128)(2,1)S(1)}, u32[]{:S(2)}, u32[]{:S(2)}) collective-permute-start(bf16[2,528,256]{2,1,0:T(8,128)(2,1)S(1)} %pad_maximum_fusion.2.refs_0_), channel_id=1, source_target_pairs={{0,3},{1,2},{2,1},{3,0},{4,7},{5,6},{6,5},{7,4},{8,11},{9,10},{10,... | collective-permute-start | bytes 1622024 | tf_op jit(solution)/shard_map/ppermute | solution.py:263
  675.9 31.7 %collective-permute-start.53 = (bf16[2,528,256]{2,1,0:T(8,128)(2,1)S(1)}, bf16[2,528,256]{2,1,0:T(8,128)(2,1)S(1)}, u32[]{:S(2)}, u32[]{:S(2)}) collective-permute-start(bf16[2,528,256]{2,1,0:T(8,128)(2,1)S(1)} %pad_maximum_fusion.3.refs_0_), channel_id=1, source_target_pairs={{0,1},{1,0},{2,3},{3,2},{4,5},{5,4},{6,7},{7,6},{8,9},{9,8},{10,11... | collective-permute-start | bytes 1622024 | tf_op jit(solution)/shard_map/ppermute | solution.py:263
  678.4 43.9 %collective-permute-start.54 = (bf16[2,528,256]{2,1,0:T(8,128)(2,1)S(1)}, bf16[2,528,256]{2,1,0:T(8,128)(2,1)S(1)}, u32[]{:S(2)}, u32[]{:S(2)}) collective-permute-start(bf16[2,528,256]{2,1,0:T(8,128)(2,1)S(1)} %pad_maximum_fusion.3.refs_0_), channel_id=1, source_target_pairs={{0,2},{1,3},{2,0},{3,1},{4,6},{5,7},{6,4},{7,5},{8,10},{9,11},{10,... | collective-permute-start | bytes 1622024 | tf_op jit(solution)/shard_map/ppermute | solution.py:263
  684.4 40.3 %collective-permute-start.55 = (bf16[2,528,256]{2,1,0:T(8,128)(2,1)S(1)}, bf16[2,528,256]{2,1,0:T(8,128)(2,1)S(1)}, u32[]{:S(2)}, u32[]{:S(2)}) collective-permute-start(bf16[2,528,256]{2,1,0:T(8,128)(2,1)S(1)} %pad_maximum_fusion.3.refs_0_), channel_id=1, source_target_pairs={{0,3},{1,2},{2,1},{3,0},{4,7},{5,6},{6,5},{7,4},{8,11},{9,10},{10,... | collective-permute-start | bytes 1622024 | tf_op jit(solution)/shard_map/ppermute | solution.py:263
  699.1 31.8 %collective-permute-start.58 = (bf16[2,528,256]{2,1,0:T(8,128)(2,1)S(1)}, bf16[2,528,256]{2,1,0:T(8,128)(2,1)S(1)}, u32[]{:S(2)}, u32[]{:S(2)}) collective-permute-start(bf16[2,528,256]{2,1,0:T(8,128)(2,1)S(1)} %pad_maximum_fusion.4.refs_0_), channel_id=1, source_target_pairs={{0,1},{1,0},{2,3},{3,2},{4,5},{5,4},{6,7},{7,6},{8,9},{9,8},{10,11... | collective-permute-start | bytes 1622024 | tf_op jit(solution)/shard_map/ppermute | solution.py:263
  701.6 43.9 %collective-permute-start.59 = (bf16[2,528,256]{2,1,0:T(8,128)(2,1)S(1)}, bf16[2,528,256]{2,1,0:T(8,128)(2,1)}, u32[]{:S(2)}, u32[]{:S(2)}) collective-permute-start(bf16[2,528,256]{2,1,0:T(8,128)(2,1)S(1)} %pad_maximum_fusion.4.refs_0_), channel_id=1, source_target_pairs={{0,2},{1,3},{2,0},{3,1},{4,6},{5,7},{6,4},{7,5},{8,10},{9,11},{10,... | collective-permute-start | bytes 1622024 | tf_op jit(solution)/shard_map/ppermute | solution.py:263
  707.6 40.4 %collective-permute-start.60 = (bf16[2,528,256]{2,1,0:T(8,128)(2,1)S(1)}, bf16[2,528,256]{2,1,0:T(8,128)(2,1)}, u32[]{:S(2)}, u32[]{:S(2)}) collective-permute-start(bf16[2,528,256]{2,1,0:T(8,128)(2,1)S(1)} %pad_maximum_fusion.4.refs_0_), channel_id=1, source_target_pairs={{0,3},{1,2},{2,1},{3,0},{4,7},{5,6},{6,5},{7,4},{8,11},{9,10},{10,... | collective-permute-start | bytes 1622024 | tf_op jit(solution)/shard_map/ppermute | solution.py:263
  722.2 31.8 %collective-permute-start.63 = (bf16[2,528,256]{2,1,0:T(8,128)(2,1)S(1)}, bf16[2,528,256]{2,1,0:T(8,128)(2,1)S(1)}, u32[]{:S(2)}, u32[]{:S(2)}) collective-permute-start(bf16[2,528,256]{2,1,0:T(8,128)(2,1)S(1)} %pad_maximum_fusion.5.refs_0_), channel_id=1, source_target_pairs={{0,1},{1,0},{2,3},{3,2},{4,5},{5,4},{6,7},{7,6},{8,9},{9,8},{10,11... | collective-permute-start | bytes 1622024 | tf_op jit(solution)/shard_map/ppermute | solution.py:263
  724.7 49.8 %collective-permute-start.64 = (bf16[2,528,256]{2,1,0:T(8,128)(2,1)S(1)}, bf16[2,528,256]{2,1,0:T(8,128)(2,1)}, u32[]{:S(2)}, u32[]{:S(2)}) collective-permute-start(bf16[2,528,256]{2,1,0:T(8,128)(2,1)S(1)} %pad_maximum_fusion.5.refs_0_), channel_id=1, source_target_pairs={{0,2},{1,3},{2,0},{3,1},{4,6},{5,7},{6,4},{7,5},{8,10},{9,11},{10,... | collective-permute-start | bytes 1622024 | tf_op jit(solution)/shard_map/ppermute | solution.py:263
  731.7 42.8 %collective-permute-start.65 = (bf16[2,528,256]{2,1,0:T(8,128)(2,1)S(1)}, bf16[2,528,256]{2,1,0:T(8,128)(2,1)}, u32[]{:S(2)}, u32[]{:S(2)}) collective-permute-start(bf16[2,528,256]{2,1,0:T(8,128)(2,1)S(1)} %pad_maximum_fusion.5.refs_0_), channel_id=1, source_target_pairs={{0,3},{1,2},{2,1},{3,0},{4,7},{5,6},{6,5},{7,4},{8,11},{9,10},{10,... | collective-permute-start | bytes 1622024 | tf_op jit(solution)/shard_map/ppermute | solution.py:263
  745.5 62.9 %collective-permute-start.28 = (bf16[2,528,128]{2,1,0:T(8,128)(2,1)S(1)}, bf16[2,528,128]{2,1,0:T(8,128)(2,1)}, u32[]{:S(2)}, u32[]{:S(2)}) collective-permute-start(bf16[2,528,128]{2,1,0:T(8,128)(2,1)S(1)} %pad_maximum_fusion.6.refs_0_), channel_id=1, source_target_pairs={{0,1},{1,0},{2,3},{3,2},{4,5},{5,4},{6,7},{7,6},{8,9},{9,8},{10,11... | collective-permute-start | bytes 811016 | tf_op jit(solution)/shard_map/ppermute | solution.py:263
  748.0 60.5 %collective-permute-start.29 = (bf16[2,528,128]{2,1,0:T(8,128)(2,1)S(1)}, bf16[2,528,128]{2,1,0:T(8,128)(2,1)}, u32[]{:S(2)}, u32[]{:S(2)}) collective-permute-start(bf16[2,528,128]{2,1,0:T(8,128)(2,1)S(1)} %pad_maximum_fusion.6.refs_0_), channel_id=1, source_target_pairs={{0,2},{1,3},{2,0},{3,1},{4,6},{5,7},{6,4},{7,5},{8,10},{9,11},{10,... | collective-permute-start | bytes 811016 | tf_op jit(solution)/shard_map/ppermute | solution.py:263
  754.0 54.4 %collective-permute-start.30 = (bf16[2,528,128]{2,1,0:T(8,128)(2,1)S(1)}, bf16[2,528,128]{2,1,0:T(8,128)(2,1)}, u32[]{:S(2)}, u32[]{:S(2)}) collective-permute-start(bf16[2,528,128]{2,1,0:T(8,128)(2,1)S(1)} %pad_maximum_fusion.6.refs_0_), channel_id=1, source_target_pairs={{0,3},{1,2},{2,1},{3,0},{4,7},{5,6},{6,5},{7,4},{8,11},{9,10},{10,... | collective-permute-start | bytes 811016 | tf_op jit(solution)/shard_map/ppermute | solution.py:263
  774.5 30.5 %collective-permute-start.34 = (bf16[2,528,128]{2,1,0:T(8,128)(2,1)S(1)}, bf16[2,528,128]{2,1,0:T(8,128)(2,1)}, u32[]{:S(2)}, u32[]{:S(2)}) collective-permute-start(bf16[2,528,128]{2,1,0:T(8,128)(2,1)S(1)} %pad_maximum_fusion.7.refs_0_), channel_id=1, source_target_pairs={{0,2},{1,3},{2,0},{3,1},{4,6},{5,7},{6,4},{7,5},{8,10},{9,11},{10,... | collective-permute-start | bytes 811016 | tf_op jit(solution)/shard_map/ppermute | solution.py:263
  774.5 30.5 %collective-permute-start.35 = (bf16[2,528,128]{2,1,0:T(8,128)(2,1)S(1)}, bf16[2,528,128]{2,1,0:T(8,128)(2,1)}, u32[]{:S(2)}, u32[]{:S(2)}) collective-permute-start(bf16[2,528,128]{2,1,0:T(8,128)(2,1)S(1)} %pad_maximum_fusion.7.refs_0_), channel_id=1, source_target_pairs={{0,3},{1,2},{2,1},{3,0},{4,7},{5,6},{6,5},{7,4},{8,11},{9,10},{10,... | collective-permute-start | bytes 811016 | tf_op jit(solution)/shard_map/ppermute | solution.py:263
  (63 other events, 3734.2 us)
